TPU v7x, 32 devices: a whole 2x2x4 slice. The times are simulated.
32 devices in a mesh: harm: 4 (over x, core), gx: 8 (over z, y).
Axes of the slice: x: 2, y: 2, z: 4, core: 2. Of those that a mesh axis runs over, the one named last changes fastest.
Arguments:
- states: bfloat16 [16, 16, 5, 2, 8, 128], P('harm', 'gx'), may hold values from -6 to 6
- jacobian: bfloat16 [31, 16, 5, 5, 2, 128], P(None, 'gx'), may hold values from -0.5 to 0.5
- source: bfloat16 [16, 5, 5, 128], P('gx'), may hold values from -2.5 to 2.5
- coupling: int32 [16, 16], replicated, may hold values from 0 to 30
- harmonic_of_slot: int32 [16], replicated, may hold values from 0 to 15, each once
Outputs:
- response: bfloat16 [16, 16, 5, 2, 8, 128], P('harm', 'gx')
Inputs may be any that keep to these rules, and one draw needn't show every extreme that they name: `harmonic_of_slot`: each harmonic appears in exactly one slot.
All inputs are finite; a program needn't handle non-finite values.
Results may differ from a plain program's by a relative error of at most 0.0038.
Values may be sent and summed in bfloat16 or wider, within the bound.
No kernel may reach another device: no remote copies, remote signals or barrier semaphores. Data moves between devices by JAX's collectives and lax.ppermute only.
A program may use at most 64 MiB of HBM per device.

v0:
```python
import jax
import jax.numpy as jnp
from jax import lax
from jax.sharding import PartitionSpec as P

H = 16


def padded_2(block, sides, width):
    for axis, dim in sides:
        count = lax.axis_size(axis)
        forward = [(i, i + 1) for i in range(count - 1)]
        forward.append((count - 1, 0))
        backward = [(target, source) for source, target in forward]
        low = lax.ppermute(
            lax.slice_in_dim(block, block.shape[dim] - width, None, axis=dim), axis, forward
        )
        high = lax.ppermute(lax.slice_in_dim(block, 0, width, axis=dim), axis, backward)
        block = jnp.concatenate([low, block, high], axis=dim)
    return block


def pair_term(jacobian_block, state_block):
    mat_real = jacobian_block[:, :, :, 0]
    mat_imag = jacobian_block[:, :, :, 1]
    vec_real = state_block[:, :, 0]
    vec_imag = state_block[:, :, 1]

    def contract(matrix, vector):
        return jnp.einsum("xaby,xbcy->xacy", matrix, vector, preferred_element_type=jnp.float32)

    real_part = contract(mat_real, vec_real) - contract(mat_imag, vec_imag)
    imag_part = contract(mat_real, vec_imag) + contract(mat_imag, vec_real)
    return jnp.stack([real_part, imag_part], axis=2)


def make_links(coupling, harmonic_of_slot, harm_index, own_count):
    own_harm = lax.dynamic_slice_in_dim(harmonic_of_slot, harm_index * own_count, own_count)
    harm_total = coupling.shape[0]
    onehot_rows = (own_harm[:, None] == jnp.arange(harm_total, dtype=jnp.int32)[None, :]).astype(
        jnp.int32
    )
    link_rows = jnp.sum(onehot_rows[:, :, None] * coupling[None, :, :], axis=1)
    return (own_harm, link_rows)


def fold_states(carry_init, block_states, jacobian, harmonic_of_slot, link_rows):
    member_count = block_states.shape[0]
    own_count = link_rows.shape[0]

    def accumulate(member, carry_sum):
        state_block = lax.dynamic_index_in_dim(block_states, member, 0, keepdims=False)
        peer_harmonic = lax.dynamic_index_in_dim(harmonic_of_slot, member, 0, keepdims=False)
        updated = []
        for own_slot in range(own_count):
            link_index = lax.dynamic_index_in_dim(
                link_rows[own_slot], peer_harmonic, 0, keepdims=False
            )
            jacobian_block = lax.dynamic_index_in_dim(jacobian, link_index, 0, keepdims=False)
            updated.append(carry_sum[own_slot] + pair_term(jacobian_block, state_block))
        return jnp.stack(updated, axis=0)

    return lax.fori_loop(0, member_count, accumulate, carry_init)


def shards(states, jacobian, source, coupling, harmonic_of_slot):
    own_count = states.shape[0]
    harm_index = lax.axis_index("harm")
    own_harm, link_rows = make_links(coupling, harmonic_of_slot, harm_index, own_count)
    initial = jnp.zeros(states.shape, jnp.float32)
    summed = fold_states(
        initial,
        lax.all_gather(states, "harm", axis=0, tiled=True),
        jacobian,
        harmonic_of_slot,
        link_rows,
    )
    flux_field = summed.astype(jnp.bfloat16)
    padded = padded_2(flux_field, (("gx", 1),), 2).astype(jnp.float32)
    divergence = (
        8.0 * (padded[:, 3:-1] - padded[:, 1:-3]) - (padded[:, 4:] - padded[:, :-4])
    ) / 12.0
    spin_rate = (own_harm.astype(jnp.float32) / H).reshape(own_count, 1, 1, 1, 1)
    imag_values = states[:, :, :, 1].astype(jnp.float32)
    real_values = states[:, :, :, 0].astype(jnp.float32)
    spin_term = jnp.stack([-spin_rate * imag_values, spin_rate * real_values], axis=3)
    merged = states.reshape(own_count, states.shape[1], 5, 2 * states.shape[4], states.shape[5])
    source_term = jnp.einsum(
        "xaby,sxbky->sxaky", source, merged, preferred_element_type=jnp.float32
    ).reshape(states.shape)
    return (divergence + spin_term + source_term).astype(jnp.bfloat16)


def solution(mesh):
    return jax.shard_map(
        shards,
        mesh=mesh,
        in_specs=(
            P("harm", "gx", None, None, None, None),
            P(None, "gx", None, None, None, None),
            P("gx", None, None, None),
            P(),
            P(),
        ),
        out_specs=P("harm", "gx", None, None, None, None),
        check_vma=False,
    )
```

profile of v0, /device:TPU:0, one launch (start us, length us, event | category | flops | bytes accessed | tf_op | source)
XLA Modules:
  0.0 906.3 jit_solution(1643764806451822669)
XLA Ops:
  0.0 11.6 %all_gather.3 = bf16[16,2,5,2,8,128]{5,4,3,2,1,0:T(8,128)(2,1)} all-gather(bf16[4,2,5,2,8,128]{5,4,3,2,1,0:T(8,128)(2,1)} %param.7), channel_id=1, replica_groups=mesh['harm'=4,'gx'=8] {'harm'}, dimensions={0}, use_global_device_ids=true | all-gather | bytes 819200 | tf_op jit(solution)/shard_map/all_gather | solution.py:73
  13.4 24.8 %copy.40 = bf16[31,2,5,5,2,128]{3,2,5,1,4,0:T(8,128)(2,1)} copy(bf16[31,2,5,5,2,128]{5,4,3,2,1,0:T(2,128)(2,1)} %param.8) | data formatting | bytes 1587200 | tf_op jit(solution)/shard_map/while | solution.py:63
  38.9 850.8 %while.13 = (s32[]{:T(128)}, f32[4,2,5,2,8,128]{5,4,3,2,1,0:T(8,128)S(1)}, bf16[16,2,5,2,8,128]{5,4,3,2,1,0:T(8,128)(2,1)}, s32[4,16]{1,0:T(4,128)}, s32[16]{0:T...) while((s32[]{:T(128)}, ...), condition=%wide.region_2.3_spmd, body=%wide.region_1.2_spmd.sunk | while | flops 2129937 | bytes 28484448 | solution.py:63
  51.2 4.4 dynamic-slice_bitcast_fusion.5
  104.4 4.4 dynamic-slice_bitcast_fusion.5
  157.6 4.4 dynamic-slice_bitcast_fusion.5
  170.3 2.5 fusion.48
  210.7 4.4 dynamic-slice_bitcast_fusion.5
  263.9 4.4 dynamic-slice_bitcast_fusion.5
  317.1 4.4 dynamic-slice_bitcast_fusion.5
  370.3 4.4 dynamic-slice_bitcast_fusion.5
  423.5 4.4 dynamic-slice_bitcast_fusion.5
  476.7 4.4 dynamic-slice_bitcast_fusion.5
  529.8 4.4 dynamic-slice_bitcast_fusion.5
  583.0 4.4 dynamic-slice_bitcast_fusion.5
  636.2 4.4 dynamic-slice_bitcast_fusion.5
  689.3 4.4 dynamic-slice_bitcast_fusion.5
  742.5 4.4 dynamic-slice_bitcast_fusion.5
  795.7 4.4 dynamic-slice_bitcast_fusion.5
  848.9 4.4 dynamic-slice_bitcast_fusion.5
  889.8 4.6 collective-permute-start.1
  895.1 3.8 copy.41
  899.9 2.6 convolution_bitcast_fusion
  902.6 2.7 copy.43
  (532 shorter events, 637.7 us)
Async XLA Ops:
  12.8 0.6 copy-start.2
  13.4 24.8 %copy-start.1 = (s32[16,16]{1,0:T(8,128)S(1)}, s32[16,16]{1,0:T(8,128)}, u32[]{:S(2)}) copy-start(s32[16,16]{1,0:T(8,128)} %param.10) | copy-start | bytes 3076
  889.8 15.6 %collective-permute-start.1 = (bf16[4,2,5,2,8,128]{5,4,3,2,1,0:T(8,128)(2,1)S(1)}, bf16[4,2,5,2,8,128]{5,4,3,2,1,0:T(8,128)(2,1)S(1)}, u32[]{:S(2)}, u32[]{:S(2)}) collective-permute-start(bf16[4,2,5,2,8,128]{5,4,3,2,1,0:T(8,128)(2,1)S(1)} %convert_element_type.28), channel_id=1, source_target_pairs={{1,0},{2,1},{3,2},{4,3},{5,4},{6,5},{7,6},{0,7},{9,8},{10,9},{11,1... | collective-permute-start | bytes 491528 | tf_op jit(solution)/shard_map/ppermute | solution.py:18
  894.4 11.0 %collective-permute-start = (bf16[4,2,5,2,8,128]{5,4,3,2,1,0:T(8,128)(2,1)S(1)}, bf16[4,2,5,2,8,128]{5,4,3,2,1,0:T(8,128)(2,1)S(1)}, u32[]{:S(2)}, u32[]{:S(2)}) collective-permute-start(bf16[4,2,5,2,8,128]{5,4,3,2,1,0:T(8,128)(2,1)S(1)} %convert_element_type.28), channel_id=1, source_target_pairs={{0,1},{1,2},{2,3},{3,4},{4,5},{5,6},{6,7},{7,0},{8,9},{9,10},{10,1... | collective-permute-start | bytes 491528 | tf_op jit(solution)/shard_map/ppermute | solution.py:15
  899.9 5.4 copy-start
  899.9 5.4 copy-start.3
where the time goes:
time: 923 us; the launch traced here: 906 us
  local copies, waits for them, and re-layouts  387 us (42%)
  matrix products  338 us (37%)
  loops' own time  146 us (16%)
  other arithmetic  18.7 us (2%)
  blocking collectives  11.6 us (1%)
    dot_general x256, matrix products, contract(): jnp.einsum('xaby,xbcy->xacy', matrix, vector, preferred_element_type=jnp....  336 us
    another operation x128, local copies, waits for them, and re-layouts, pair_term(): return jnp.stack([real_part, imag_part], axis=2)  210 us
    another operation x1, loops' own time, fold_states(): return lax.fori_loop(0, member_count, accumulate, carry_init)  146 us
    squeeze x16, local copies, waits for them, and re-layouts, accumulate(): lax.dynamic_index_in_dim(jacobian, link_index, 0, keepdims=False)  69.8 us
    while x1, local copies, waits for them, and re-layouts, fold_states(): return lax.fori_loop(0, member_count, accumulate, carry_init)  24.8 us
    dynamic_slice x32, local copies, waits for them, and re-layouts, accumulate(): lax.dynamic_index_in_dim(block_states, member, 0, keepdims=False)  22 us
    dynamic_slice x16, local copies, waits for them, and re-layouts, accumulate(): lax.dynamic_index_in_dim(harmonic_of_slot, member, 0, keepdims=False)  19.8 us
    dynamic_slice x32, local copies, waits for them, and re-layouts, accumulate(): lax.dynamic_index_in_dim(link_rows[own_slot], peer_harmonic, 0, keepdims=...  19 us
  transfers between devices with their start and end apart: 2, of which 0 were waited for; matrix products, arithmetic and copies ran while one was open for 1% of the time, Pallas kernels for 0%

commit v1 on v0

v1 whole, which is shorter than its diff:
```python
import functools

import jax
import jax.numpy as jnp
from jax import lax
from jax.experimental import pallas as pl
from jax.experimental.pallas import tpu as pltpu
from jax.sharding import PartitionSpec as P

VMEM = pltpu.VMEM
SMEM = pltpu.SMEM
VARS = 5


def row(table, index):
    return table[pl.ds(index, 8, stride=0), :]


def expand(jac_ref, table, sums):
    count = jac_ref.shape[0] // 2
    table[: 2 * count, :] = jac_ref[...].astype(jnp.float32)
    for start in range(0, count, 8):
        size = min(8, count - start)
        real = table[pl.ds(2 * start, size, stride=2), :]
        imag = table[pl.ds(2 * start + 1, size, stride=2), :]
        sums[pl.ds(start, size), :] = real + imag


def flux_block(first_own, first_peer, harm_ref, coup_ref, state_ref, table, sums, own, cell, cells, acc):
    def body(member, acc):
        peer = harm_ref[first_peer + member]
        vec_real, vec_imag, vec_sum = [], [], []
        for b in range(VARS):
            both = state_ref[member, cell, b].astype(jnp.float32)
            vec_real.append(both[0])
            vec_imag.append(both[1])
            vec_sum.append(both[0] + both[1])
        out = []
        for place, slot in enumerate(own):
            link = coup_ref[harm_ref[first_own + slot], peer]
            base = (link * cells + cell) * (VARS * VARS)
            part = list(acc[place])
            for a in range(VARS):
                for b in range(VARS):
                    offset = a * VARS + b
                    part[3 * a] += row(table, 2 * (base + offset)) * vec_real[b]
                    part[3 * a + 1] += row(table, 2 * (base + offset) + 1) * vec_imag[b]
                    part[3 * a + 2] += row(sums, base + offset) * vec_sum[b]
            out.append(tuple(part))
        return tuple(out)

    return lax.fori_loop(0, state_ref.shape[0], body, acc)


def flux_kernel(groups, stage, *refs):
    harm_ref, coup_ref = refs[:2]
    refs = refs[2:]
    harm = lax.axis_index("harm")
    states = refs[: len(groups)]
    refs = refs[len(groups) :]
    if stage == 0:
        jac_ref, out_ref, table, sums = refs
        expand(jac_ref, table, sums)
        start_ref = None
    else:
        table, sums, start_ref, out_ref = refs
    own_count, cells = out_ref.shape[:2]
    width = 2 if own_count % 2 == 0 else 1
    zero = jnp.zeros((8, 128), jnp.float32)

    def chunk(step, _):
        cell = step % cells
        first = (step // cells) * width
        acc = tuple((zero,) * (3 * VARS) for _ in range(width))
        for shift, state_ref in zip(groups, states):
            peer_group = harm ^ shift
            acc = flux_block(
                harm * own_count + first, peer_group * own_count, harm_ref, coup_ref, state_ref,
                table, sums, range(width), cell, cells, acc,
            )
        for place in range(width):
            for a in range(VARS):
                one, two, three = acc[place][3 * a : 3 * a + 3]
                real = one - two
                imag = three - one - two
                if start_ref is not None:
                    real = real + start_ref[first + place, cell, a, 0]
                    imag = imag + start_ref[first + place, cell, a, 1]
                out_ref[first + place, cell, a, 0] = real.astype(out_ref.dtype)
                out_ref[first + place, cell, a, 1] = imag.astype(out_ref.dtype)
        return 0

    lax.fori_loop(0, cells * (own_count // width), chunk, 0)


def final_kernel(harm_total, harm_ref, own_ref, near_ref, far_ref, state_ref, source_ref, out_ref, table):
    own_count, cells = own_ref.shape[:2]
    harm = lax.axis_index("harm")
    gx = lax.axis_index("gx")
    table[: source_ref.shape[0], :] = source_ref[...].astype(jnp.float32)

    def finish(left_ref, right_ref):
        def flux(slot, a, place):
            if place < 0:
                return left_ref[slot, cells + place, a].astype(jnp.float32)
            if place >= cells:
                return right_ref[slot, place - cells, a].astype(jnp.float32)
            return own_ref[slot, place, a].astype(jnp.float32)

        def body(slot, _):
            spin = harm_ref[harm * own_count + slot].astype(jnp.float32) / harm_total
            for cell in range(cells):
                vec = [state_ref[slot, cell, b].astype(jnp.float32) for b in range(VARS)]
                for a in range(VARS):
                    total = (
                        8.0 * (flux(slot, a, cell + 1) - flux(slot, a, cell - 1))
                        - (flux(slot, a, cell + 2) - flux(slot, a, cell - 2))
                    ) / 12.0
                    real, imag = total[0], total[1]
                    real = real - spin * vec[a][1]
                    imag = imag + spin * vec[a][0]
                    for b in range(VARS):
                        weight = row(table, (cell * VARS + a) * VARS + b)
                        real = real + weight * vec[b][0]
                        imag = imag + weight * vec[b][1]
                    out_ref[slot, cell, a, 0] = real.astype(out_ref.dtype)
                    out_ref[slot, cell, a, 1] = imag.astype(out_ref.dtype)
            return 0

        lax.fori_loop(0, own_count, body, 0)

    @pl.when(gx % 2 == 0)
    def _():
        finish(far_ref, near_ref)

    @pl.when(gx % 2 == 1)
    def _():
        finish(near_ref, far_ref)


def call(kernel, out, spaces, scratch, name):
    return pl.pallas_call(
        kernel,
        out_shape=out,
        in_specs=[pl.BlockSpec(memory_space=space) for space in spaces],
        out_specs=jax.tree.map(lambda _: pl.BlockSpec(memory_space=VMEM), out),
        scratch_shapes=scratch,
        name=name,
    )


def shards(states, jacobian, source, coupling, harmonic_of_slot):
    own_count, cells = states.shape[:2]
    harms = lax.axis_size("harm")
    planes = lax.axis_size("gx")
    pairs = jacobian.shape[0] * cells * VARS * VARS

    def swap(block, shift):
        return lax.ppermute(block, "harm", [(i, i ^ shift) for i in range(harms)])

    held = {0: states}
    for shift in range(1, harms):
        low = shift & -shift
        held[shift] = swap(states if shift == low else held[shift ^ low], low if shift != low else shift)
    first = [0, 1]
    rest = [shift for shift in range(2, harms)]
    flat = jacobian.reshape(2 * pairs, 128)
    f32 = jnp.float32
    part, table, sums = call(
        functools.partial(flux_kernel, first, 0),
        (
            jax.ShapeDtypeStruct(states.shape, f32),
            jax.ShapeDtypeStruct((2 * pairs + 8, 128), f32),
            jax.ShapeDtypeStruct((pairs + 8, 128), f32),
        ),
        [SMEM, SMEM] + [VMEM] * 3,
        [],
        "flux_a",
    )(harmonic_of_slot, coupling, *[held[s] for s in first], flat)
    flux = call(
        functools.partial(flux_kernel, rest, 1),
        jax.ShapeDtypeStruct(states.shape, jnp.bfloat16),
        [SMEM, SMEM] + [VMEM] * (len(rest) + 3),
        [],
        "flux_b",
    )(harmonic_of_slot, coupling, *[held[s] for s in rest], table, sums, part)
    near_pairs = [(i, i ^ 1) for i in range(planes)]
    far_pairs = [(i, (i + 1) % planes if i % 2 else (i - 1) % planes) for i in range(planes)]
    far = lax.ppermute(flux, "gx", far_pairs)
    near = lax.ppermute(flux, "gx", near_pairs)
    return call(
        functools.partial(final_kernel, coupling.shape[0]),
        jax.ShapeDtypeStruct(states.shape, jnp.bfloat16),
        [SMEM] + [VMEM] * 5,
        [pltpu.VMEM((cells * VARS * VARS + 8, 128), f32)],
        "finish",
    )(harmonic_of_slot, flux, near, far, states, source.reshape(cells * VARS * VARS, 128))


def solution(mesh):
    return jax.shard_map(
        shards,
        mesh=mesh,
        in_specs=(
            P("harm", "gx", None, None, None, None),
            P(None, "gx", None, None, None, None),
            P("gx", None, None, None),
            P(),
            P(),
        ),
        out_specs=P("harm", "gx", None, None, None, None),
        check_vma=False,
    )
```

time: 923 us -> 35.1 us (0.04); the launches traced: 906 us -> 34.9 us
  local copies, waits for them, and re-layouts: 387 us -> 5.67 us
  matrix products: 338 us -> 0 us
  loops' own time: 146 us -> 0 us
  other arithmetic: 18.7 us -> 0 us
  blocking collectives: 11.6 us -> 0 us
  Pallas kernels: 0 us -> 11.5 us
  waiting for transfers between devices: 0.01 us -> 9.41 us
    dot_general x257 -> x0, matrix products: 338 us -> none  [the longest x256 336 us: contract(): jnp.einsum('xaby,xbcy->xacy', matrix, vector, preferred_element_type=jnp....]
    another operation x128 -> x0, local copies, waits for them, and re-layouts: 210 us -> none  [pair_term(): return jnp.stack([real_part, imag_part], axis=2)]
    another operation x1 -> x0, loops' own time: 146 us -> none  [fold_states(): return lax.fori_loop(0, member_count, accumulate, carry_init)]
    squeeze x16 -> x0, local copies, waits for them, and re-layouts: 69.8 us -> none  [accumulate(): lax.dynamic_index_in_dim(jacobian, link_index, 0, keepdims=False)]
    dynamic_slice x80 -> x0, local copies, waits for them, and re-layouts: 60.7 us -> none  [the longest x32 22 us: accumulate(): lax.dynamic_index_in_dim(block_states, member, 0, keepdims=False)]
    while x1 -> x0, local copies, waits for them, and re-layouts: 24.8 us -> none  [fold_states(): return lax.fori_loop(0, member_count, accumulate, carry_init)]
    add x16 -> x0, other arithmetic: 14.7 us -> none  [accumulate(): updated.append(carry_sum[own_slot] + pair_term(jacobian_block, state_block))]
    slice x16 -> x0, local copies, waits for them, and re-layouts: 13.2 us -> none  [accumulate(): link_rows[own_slot]]
  transfers between devices with their start and end apart: 2 -> 5, of which waited for: 0 -> 3; matrix products, arithmetic and copies ran while one was open for 1% -> 10% of each run, Pallas kernels for 0% -> 14%
where the time goes in v1:
time: 35.1 us; the launch traced here: 34.9 us
  Pallas kernels  11.5 us (33%)
  waiting for transfers between devices  9.41 us (27%)
  starting transfers between devices  8.29 us (24%)
  local copies, waits for them, and re-layouts  5.67 us (16%)
    pallas_call x1, Pallas kernels, shards(): call(functools.partial(flux_kernel, first, 0), (jax.ShapeDtypeStruct(stat...  4.95 us
    pallas_call x1, Pallas kernels, shards(): call(functools.partial(flux_kernel, rest, 1), jax.ShapeDtypeStruct(states...  4.45 us
    ppermute x3, waiting for transfers between devices, swap(): return lax.ppermute(block, 'harm', [(i, i ^ shift) for i in range(harms)])  4.41 us
    ppermute x1, waiting for transfers between devices, shards(): near = lax.ppermute(flux, 'gx', near_pairs)  3.73 us
    ppermute x1, starting transfers between devices, shards(): far = lax.ppermute(flux, 'gx', far_pairs)  3.54 us
    reshape x1, local copies, waits for them, and re-layouts, shards(): flat = jacobian.reshape(2 * pairs, 128)  3.03 us
    ppermute x3, starting transfers between devices, swap(): return lax.ppermute(block, 'harm', [(i, i ^ shift) for i in range(harms)])  2.97 us
    pallas_call x1, Pallas kernels, shards(): call(functools.partial(final_kernel, coupling.shape[0]), jax.ShapeDtypeSt...  2.11 us
  transfers between devices with their start and end apart: 5, of which 3 were waited for; matrix products, arithmetic and copies ran while one was open for 10% of the time, Pallas kernels for 14%

profile of v1, /device:TPU:0, one launch (start us, length us, event | category | flops | bytes accessed | tf_op | source)
XLA Modules:
  0.0 34.9 jit_solution(14356056667625192607)
XLA Ops:
  0.0 3.0 %collective-permute-start = (bf16[4,2,5,2,8,128]{5,4,3,2,1,0:T(8,128)(2,1)}, bf16[4,2,5,2,8,128]{5,4,3,2,1,0:T(8,128)(2,1)S(1)}, u32[]{:S(2)}, u32[]{:S(2)}) collective-permute-start(bf16[4,2,5,2,8,128]{5,4,3,2,1,0:T(8,128)(2,1)} %state_ref.1), channel_id=1, source_target_pairs={{0,16},{8,24},{16,0},{24,8},{1,17},{9,25},{17,1},{25,9},{2,18},{10... | collective-permute-start | bytes 491528 | tf_op jit(solution)/shard_map/ppermute | solution.py:159
  3.0 0.0 collective-permute-start.2
  3.0 4.4 %collective-permute-done.refs_2_ = bf16[4,2,5,2,8,128]{5,4,3,2,1,0:T(8,128)(2,1)S(1)} collective-permute-done((bf16[4,2,5,2,8,128]{5,4,3,2,1,0:T(8,128)(2,1)}, bf16[4,2,5,2,8,128]{5,4,3,2,1,0:T(8,128)(2,1)S(1)}, u32[]{:S(2)}, u32[]{:S(2)}) %collective-permute-start) | collective-permute-done | bytes 163872 | tf_op jit(solution)/shard_map/ppermute | solution.py:159
  7.4 0.0 copy-start.2
  7.4 0.0 collective-permute-start.1
  7.4 3.0 %reshape.6.refs_4_ = bf16[3100,128]{1,0:T(8,128)(2,1)} reshape(bf16[31,2,5,5,2,128]{5,4,3,2,1,0:T(2,128)(2,1)} %param.6) | data formatting | bytes 1587200 | tf_op jit(solution)/shard_map/reshape | solution.py:167
  10.4 0.0 collective-permute-done.2.refs_3_
  10.4 0.0 copy-start.4
  10.4 0.7 %copy-done.4 = bf16[4,2,5,2,8,128]{5,4,3,2,1,0:T(8,128)(2,1)} copy-done((bf16[4,2,5,2,8,128]{5,4,3,2,1,0:T(8,128)(2,1)}, bf16[4,2,5,2,8,128]{5,4,3,2,1,0:T(8,128)(2,1)S(1)}, u32[]{:S(2)}) %copy-start.4) | copy-done | bytes 163864
  11.1 5.0 %flux_a.1 = (f32[4,2,5,2,8,128]{5,4,3,2,1,0:T(8,128)}, f32[3108,128]{1,0:T(8,128)}, f32[1558,128]{1,0:T(8,128)}) custom-call(s32[16]{0:T(128)} %harm_ref.1, s32[16,16]{1,0:T(8,128)} %refs_1_.3, bf16[4,2,5,2,8,128]{5,4,3,2,1,0:T(8,128)(2,1)} %state_ref.1, bf16[4,2,5,2,8,128]{5,4,3,2,1,0:T(8,128)(2,1)} %copy-done.4, bf16[3100,128]{1,0:T(8,128)(2,1)} %reshape.6.refs_4_), custom_call_target="tpu_custom_call" | custom-call | tf_op jit(solution)/shard_map/flux_a/pallas_call | solution.py:169
  16.0 0.0 collective-permute-done.1.refs_3_
  16.0 0.0 copy-start.3
  16.0 0.0 copy-done.2
  16.0 0.7 %copy-done.3 = bf16[4,2,5,2,8,128]{5,4,3,2,1,0:T(8,128)(2,1)} copy-done((bf16[4,2,5,2,8,128]{5,4,3,2,1,0:T(8,128)(2,1)}, bf16[4,2,5,2,8,128]{5,4,3,2,1,0:T(8,128)(2,1)S(1)}, u32[]{:S(2)}) %copy-start.3) | copy-done | bytes 163864
  16.7 4.5 %flux_b.1.own_ref = bf16[4,2,5,2,8,128]{5,4,3,2,1,0:T(8,128)(2,1)} custom-call(s32[16]{0:T(128)} %harm_ref.1, s32[16,16]{1,0:T(8,128)} %refs_1_.3, bf16[4,2,5,2,8,128]{5,4,3,2,1,0:T(8,128)(2,1)} %copy-done.2, bf16[4,2,5,2,8,128]{5,4,3,2,1,0:T(8,128)(2,1)} %copy-done.3, f32[3108,128]{1,0:T(8,128)} %get-tuple-element.8.refs_4_, ...), custom_call_target="tpu_custom_call" | custom-call | tf_op jit(solution)/shard_map/flux_b/pallas_call | solution.py:180
  21.2 1.8 %collective-permute-start.3 = (bf16[4,2,5,2,8,128]{5,4,3,2,1,0:T(8,128)(2,1)}, bf16[4,2,5,2,8,128]{5,4,3,2,1,0:T(8,128)(2,1)S(1)}, u32[]{:S(2)}, u32[]{:S(2)}) collective-permute-start(bf16[4,2,5,2,8,128]{5,4,3,2,1,0:T(8,128)(2,1)} %flux_b.1.own_ref), channel_id=1, source_target_pairs={{0,1},{1,0},{2,3},{3,2},{4,5},{5,4},{6,7},{7,6},{8,9},{9,8},{10,11... | collective-permute-start | bytes 491528 | tf_op jit(solution)/shard_map/ppermute | solution.py:190
  22.9 3.5 %collective-permute-start.4 = (bf16[4,2,5,2,8,128]{5,4,3,2,1,0:T(8,128)(2,1)}, bf16[4,2,5,2,8,128]{5,4,3,2,1,0:T(8,128)(2,1)S(1)}, u32[]{:S(2)}, u32[]{:S(2)}) collective-permute-start(bf16[4,2,5,2,8,128]{5,4,3,2,1,0:T(8,128)(2,1)} %flux_b.1.own_ref), channel_id=1, source_target_pairs={{0,7},{1,2},{2,1},{3,4},{4,3},{5,6},{6,5},{7,0},{8,15},{9,10},{10,... | collective-permute-start | bytes 491528 | tf_op jit(solution)/shard_map/ppermute | solution.py:189
  26.5 0.0 copy-done.5
  26.5 0.6 %reshape.7.source_ref = bf16[50,128]{1,0:T(8,128)(2,1)} reshape(bf16[2,5,5,128]{3,2,1,0:T(8,128)(2,1)S(1)} %copy.7) | data formatting | bytes 25600 | tf_op jit(solution)/shard_map/reshape | solution.py:197
  27.1 3.7 %collective-permute-done.3.near_ref = bf16[4,2,5,2,8,128]{5,4,3,2,1,0:T(8,128)(2,1)S(1)} collective-permute-done((bf16[4,2,5,2,8,128]{5,4,3,2,1,0:T(8,128)(2,1)}, bf16[4,2,5,2,8,128]{5,4,3,2,1,0:T(8,128)(2,1)S(1)}, u32[]{:S(2)}, u32[]{:S(2)}) %collective-permute-start.3) | collective-permute-done | bytes 163872 | tf_op jit(solution)/shard_map/ppermute | solution.py:190
  30.8 1.3 %collective-permute-done.4.far_ref = bf16[4,2,5,2,8,128]{5,4,3,2,1,0:T(8,128)(2,1)S(1)} collective-permute-done((bf16[4,2,5,2,8,128]{5,4,3,2,1,0:T(8,128)(2,1)}, bf16[4,2,5,2,8,128]{5,4,3,2,1,0:T(8,128)(2,1)S(1)}, u32[]{:S(2)}, u32[]{:S(2)}) %collective-permute-start.4) | collective-permute-done | bytes 163872 | tf_op jit(solution)/shard_map/ppermute | solution.py:189
  32.1 0.0 copy-done
  32.1 0.7 %copy-done.1 = bf16[4,2,5,2,8,128]{5,4,3,2,1,0:T(8,128)(2,1)} copy-done((bf16[4,2,5,2,8,128]{5,4,3,2,1,0:T(8,128)(2,1)}, bf16[4,2,5,2,8,128]{5,4,3,2,1,0:T(8,128)(2,1)S(1)}, u32[]{:S(2)}) %copy-start.1) | copy-done | bytes 163864
  32.8 2.1 %finish.1 = bf16[4,2,5,2,8,128]{5,4,3,2,1,0:T(8,128)(2,1)} custom-call(s32[16]{0:T(128)} %harm_ref.1, bf16[4,2,5,2,8,128]{5,4,3,2,1,0:T(8,128)(2,1)} %flux_b.1.own_ref, bf16[4,2,5,2,8,128]{5,4,3,2,1,0:T(8,128)(2,1)} %copy-done, bf16[4,2,5,2,8,128]{5,4,3,2,1,0:T(8,128)(2,1)} %copy-done.1, bf16[4,2,5,2,8,128]{5,4,3,2,1,0:T(8,128)(2,1)} %state_ref.1, ...), custom_call_target="tpu_custom_call" | custom-call | tf_op jit(solution)/shard_map/finish/pallas_call | solution.py:191
  (4 shorter events, 0.0 us)
Async XLA Ops:
  0.0 7.4 %collective-permute-start = (bf16[4,2,5,2,8,128]{5,4,3,2,1,0:T(8,128)(2,1)}, bf16[4,2,5,2,8,128]{5,4,3,2,1,0:T(8,128)(2,1)S(1)}, u32[]{:S(2)}, u32[]{:S(2)}) collective-permute-start(bf16[4,2,5,2,8,128]{5,4,3,2,1,0:T(8,128)(2,1)} %state_ref.1), channel_id=1, source_target_pairs={{0,16},{8,24},{16,0},{24,8},{1,17},{9,25},{17,1},{25,9},{2,18},{10... | collective-permute-start | bytes 491528 | tf_op jit(solution)/shard_map/ppermute | solution.py:159
  3.0 7.4 %collective-permute-start.2 = (bf16[4,2,5,2,8,128]{5,4,3,2,1,0:T(8,128)(2,1)}, bf16[4,2,5,2,8,128]{5,4,3,2,1,0:T(8,128)(2,1)S(1)}, u32[]{:S(2)}, u32[]{:S(2)}) collective-permute-start(bf16[4,2,5,2,8,128]{5,4,3,2,1,0:T(8,128)(2,1)} %state_ref.1), channel_id=1, source_target_pairs={{0,8},{8,0},{16,24},{24,16},{1,9},{9,1},{17,25},{25,17},{2,10},{10... | collective-permute-start | bytes 491528 | tf_op jit(solution)/shard_map/ppermute | solution.py:159
  7.4 8.7 %copy-start.2 = (bf16[4,2,5,2,8,128]{5,4,3,2,1,0:T(8,128)(2,1)}, bf16[4,2,5,2,8,128]{5,4,3,2,1,0:T(8,128)(2,1)S(1)}, u32[]{:S(2)}) copy-start(bf16[4,2,5,2,8,128]{5,4,3,2,1,0:T(8,128)(2,1)S(1)} %collective-permute-done.refs_2_) | copy-start | bytes 491524
  7.4 8.7 %collective-permute-start.1 = (bf16[4,2,5,2,8,128]{5,4,3,2,1,0:T(8,128)(2,1)S(1)}, bf16[4,2,5,2,8,128]{5,4,3,2,1,0:T(8,128)(2,1)S(1)}, u32[]{:S(2)}, u32[]{:S(2)}) collective-permute-start(bf16[4,2,5,2,8,128]{5,4,3,2,1,0:T(8,128)(2,1)S(1)} %collective-permute-done.refs_2_), channel_id=1, source_target_pairs={{0,8},{8,0},{16,24},{24,16},{1,9},{9,1},{17,25},{25,17},{2,10},{10... | collective-permute-start | bytes 491528 | tf_op jit(solution)/shard_map/ppermute | solution.py:159
  10.4 0.7 %copy-start.4 = (bf16[4,2,5,2,8,128]{5,4,3,2,1,0:T(8,128)(2,1)}, bf16[4,2,5,2,8,128]{5,4,3,2,1,0:T(8,128)(2,1)S(1)}, u32[]{:S(2)}) copy-start(bf16[4,2,5,2,8,128]{5,4,3,2,1,0:T(8,128)(2,1)S(1)} %collective-permute-done.2.refs_3_) | copy-start | bytes 491524
  16.0 0.7 %copy-start.3 = (bf16[4,2,5,2,8,128]{5,4,3,2,1,0:T(8,128)(2,1)}, bf16[4,2,5,2,8,128]{5,4,3,2,1,0:T(8,128)(2,1)S(1)}, u32[]{:S(2)}) copy-start(bf16[4,2,5,2,8,128]{5,4,3,2,1,0:T(8,128)(2,1)S(1)} %collective-permute-done.1.refs_3_) | copy-start | bytes 491524
  16.7 9.8 %copy-start.5 = (bf16[2,5,5,128]{3,0,2,1:T(2,128)(2,1)S(1)}, bf16[2,5,5,128]{3,0,2,1:T(2,128)(2,1)}, u32[]{:S(2)}) copy-start(bf16[2,5,5,128]{3,0,2,1:T(2,128)(2,1)} %param.7) | copy-start | bytes 38404
  21.2 9.7 %collective-permute-start.3 = (bf16[4,2,5,2,8,128]{5,4,3,2,1,0:T(8,128)(2,1)}, bf16[4,2,5,2,8,128]{5,4,3,2,1,0:T(8,128)(2,1)S(1)}, u32[]{:S(2)}, u32[]{:S(2)}) collective-permute-start(bf16[4,2,5,2,8,128]{5,4,3,2,1,0:T(8,128)(2,1)} %flux_b.1.own_ref), channel_id=1, source_target_pairs={{0,1},{1,0},{2,3},{3,2},{4,5},{5,4},{6,7},{7,6},{8,9},{9,8},{10,11... | collective-permute-start | bytes 491528 | tf_op jit(solution)/shard_map/ppermute | solution.py:190
  22.9 9.2 %collective-permute-start.4 = (bf16[4,2,5,2,8,128]{5,4,3,2,1,0:T(8,128)(2,1)}, bf16[4,2,5,2,8,128]{5,4,3,2,1,0:T(8,128)(2,1)S(1)}, u32[]{:S(2)}, u32[]{:S(2)}) collective-permute-start(bf16[4,2,5,2,8,128]{5,4,3,2,1,0:T(8,128)(2,1)} %flux_b.1.own_ref), channel_id=1, source_target_pairs={{0,7},{1,2},{2,1},{3,4},{4,3},{5,6},{6,5},{7,0},{8,15},{9,10},{10,... | collective-permute-start | bytes 491528 | tf_op jit(solution)/shard_map/ppermute | solution.py:189
  30.8 1.3 %copy-start = (bf16[4,2,5,2,8,128]{5,4,3,2,1,0:T(8,128)(2,1)}, bf16[4,2,5,2,8,128]{5,4,3,2,1,0:T(8,128)(2,1)S(1)}, u32[]{:S(2)}) copy-start(bf16[4,2,5,2,8,128]{5,4,3,2,1,0:T(8,128)(2,1)S(1)} %collective-permute-done.3.near_ref) | copy-start | bytes 491524
  32.1 0.7 %copy-start.1 = (bf16[4,2,5,2,8,128]{5,4,3,2,1,0:T(8,128)(2,1)}, bf16[4,2,5,2,8,128]{5,4,3,2,1,0:T(8,128)(2,1)S(1)}, u32[]{:S(2)}) copy-start(bf16[4,2,5,2,8,128]{5,4,3,2,1,0:T(8,128)(2,1)S(1)} %collective-permute-done.4.far_ref) | copy-start | bytes 491524

commit v2 on v1

v2 whole, which is shorter than its diff:
```python
import functools

import jax
import jax.numpy as jnp
from jax import lax
from jax.experimental import pallas as pl
from jax.experimental.pallas import tpu as pltpu
from jax.sharding import PartitionSpec as P


VMEM = pltpu.VMEM
SMEM = pltpu.SMEM
HBM = pltpu.HBM
F32 = jnp.float32
VARS = 5
LIMIT = 16 << 20
PIECES = 4


def row(table, index):
    return table[pl.ds(index, 8, stride=0), :]


def flux_block(first_own, first_peer, harm_ref, coup_ref, state_ref, table, sums, own, cell, cells, acc):
    count = state_ref.shape[0]

    def places(member):
        peer = harm_ref[first_peer + member]
        return tuple(
            (coup_ref[harm_ref[first_own + slot], peer] * cells + cell) * (VARS * VARS) for slot in own
        )

    def body(member, carry):
        acc, bases = carry
        following = places(jnp.minimum(member + 1, count - 1))
        out = [list(part) for part in acc]
        for b in range(VARS):
            both = state_ref[member, cell, b].astype(F32)
            real, imag = both[0], both[1]
            total = real + imag
            for part, base in zip(out, bases):
                for a in range(VARS):
                    offset = base + (a * VARS + b)
                    part[3 * a] += row(table, 2 * offset) * real
                    part[3 * a + 1] += row(table, 2 * offset + 1) * imag
                    part[3 * a + 2] += row(sums, offset) * total
        return tuple(tuple(part) for part in out), following

    unroll = 2 if count % 2 == 0 else 1
    return lax.fori_loop(0, count, body, (acc, places(0)), unroll=unroll)[0]


def flux_sum(groups, states, harm_ref, coup_ref, table, sums, start_ref, out_ref):
    harm = lax.axis_index("harm")
    own_count, cells = out_ref.shape[:2]
    width = 2 if own_count % 2 == 0 else 1
    zero = jnp.zeros((8, 128), F32)

    def chunk(step, _):
        cell = step % cells
        first = (step // cells) * width
        acc = tuple((zero,) * (3 * VARS) for _ in range(width))
        for shift, state_ref in zip(groups, states):
            acc = flux_block(
                harm * own_count + first, (harm ^ shift) * own_count, harm_ref, coup_ref, state_ref,
                table, sums, range(width), cell, cells, acc,
            )
        for place in range(width):
            for a in range(VARS):
                one, two, three = acc[place][3 * a : 3 * a + 3]
                real = one - two
                imag = three - one - two
                if start_ref is not None:
                    real = real + start_ref[first + place, cell, a, 0]
                    imag = imag + start_ref[first + place, cell, a, 1]
                out_ref[first + place, cell, a, 0] = real.astype(out_ref.dtype)
                out_ref[first + place, cell, a, 1] = imag.astype(out_ref.dtype)
        return 0

    lax.fori_loop(0, cells * (own_count // width), chunk, 0)


def first_kernel(
    jac_hbm, state_hbm, harm_hbm, coup_hbm, out_ref, table, sums, harm_ref, coup_ref,
    jac, own, jac_sem, sem,
):
    rows = jac_hbm.size // 128
    flat = jac_hbm.reshape(rows, 128)
    step = -(-rows // (16 * PIECES)) * 16
    spans = [(start, min(step, rows - start)) for start in range(0, rows, step)]
    copies = [
        pltpu.make_async_copy(flat.at[pl.ds(start, size)], jac.at[pl.ds(start, size)], jac_sem.at[i])
        for i, (start, size) in enumerate(spans)
    ]
    others = [
        pltpu.make_async_copy(source, target, sem.at[i])
        for i, (source, target) in enumerate(((harm_hbm, harm_ref), (coup_hbm, coup_ref), (state_hbm, own)))
    ]
    for copy in copies + others:
        copy.start()
    for copy, (start, size) in zip(copies, spans):
        copy.wait()
        for at in range(start, start + size, 16):
            table[pl.ds(at, 16), :] = jac[pl.ds(at, 16), :].astype(F32)
        for at in range(start // 2, (start + size) // 2, 8):
            real = table[pl.ds(2 * at, 8, stride=2), :]
            imag = table[pl.ds(2 * at + 1, 8, stride=2), :]
            sums[pl.ds(at, 8), :] = real + imag
    for copy in others:
        copy.wait()
    flux_sum((0,), (own,), harm_ref, coup_ref, table, sums, None, out_ref)


def next_kernel(groups, harm_ref, coup_ref, *refs):
    states = refs[: len(groups)]
    table, sums, start_ref, out_ref = refs[len(groups) :]
    flux_sum(groups, states, harm_ref, coup_ref, table, sums, start_ref, out_ref)


def local_kernel(harm_total, harm_ref, flux_ref, state_ref, source_ref, out_ref, table):
    own_count, cells = flux_ref.shape[:2]
    first = lax.axis_index("harm") * own_count
    table[: source_ref.shape[0], :] = source_ref[...].astype(F32)

    def body(slot, _):
        spin = harm_ref[first + slot].astype(F32) / harm_total
        for cell in range(cells):
            vec = [state_ref[slot, cell, b].astype(F32) for b in range(VARS)]
            for a in range(VARS):
                real = -spin * vec[a][1]
                imag = spin * vec[a][0]
                for step, weight in ((-2, 1 / 12), (-1, -8 / 12), (1, 8 / 12), (2, -1 / 12)):
                    if 0 <= cell + step < cells:
                        other = flux_ref[slot, cell + step, a].astype(F32)
                        real = real + weight * other[0]
                        imag = imag + weight * other[1]
                for b in range(VARS):
                    weight = row(table, (cell * VARS + a) * VARS + b)
                    real = real + weight * vec[b][0]
                    imag = imag + weight * vec[b][1]
                out_ref[slot, cell, a, 0] = real
                out_ref[slot, cell, a, 1] = imag
        return 0

    lax.fori_loop(0, own_count, body, 0)


def final_kernel(local_ref, near_ref, far_ref, out_ref):
    own_count, cells = out_ref.shape[:2]

    def finish(left_ref, right_ref):
        def body(slot, _):
            for a in range(VARS):
                for cell in range(cells):
                    total = local_ref[slot, cell, a]
                    for step, weight in ((-2, 1 / 12), (-1, -8 / 12), (1, 8 / 12), (2, -1 / 12)):
                        place = cell + step
                        if place < 0:
                            total = total + weight * left_ref[slot, cells + place, a].astype(F32)
                        elif place >= cells:
                            total = total + weight * right_ref[slot, place - cells, a].astype(F32)
                    out_ref[slot, cell, a] = total.astype(out_ref.dtype)
            return 0

        lax.fori_loop(0, own_count, body, 0)

    even = lax.axis_index("gx") % 2 == 0

    @pl.when(even)
    def _():
        finish(far_ref, near_ref)

    @pl.when(jnp.logical_not(even))
    def _():
        finish(near_ref, far_ref)


def call(kernel, out, spaces, flops, scratch=()):
    return pl.pallas_call(
        kernel,
        out_shape=out,
        in_specs=[pl.BlockSpec(memory_space=space) for space in spaces],
        out_specs=jax.tree.map(lambda x: pl.BlockSpec(memory_space=getattr(x, 'memory_space', VMEM)), out),
        scratch_shapes=scratch,
        compiler_params=pltpu.CompilerParams(vmem_limit_bytes=LIMIT),
        cost_estimate=pl.CostEstimate(flops=flops, bytes_accessed=0, transcendentals=0),
    )


def body(states, jacobian, source, coupling, harmonic_of_slot):
    shape = states.shape
    own_count, cells = shape[:2]
    harms = lax.axis_size("harm")
    planes = lax.axis_size("gx")
    pairs = jacobian.shape[0] * cells * VARS * VARS
    padded = -(-2 * pairs // 16) * 16
    dma = pltpu.SemaphoreType.DMA
    shaped = jax.ShapeDtypeStruct

    def swap(block, shift):
        return lax.ppermute(block, "harm", [(i, i ^ shift) for i in range(harms)])

    work = 2 * VARS * VARS * 6 * own_count * states.size // (2 * VARS)
    even = [shift for shift in range(2, harms, 2)]
    odd = [shift + 1 for shift in even]
    partner = swap(states, 1)
    even_states = [swap(states, shift) for shift in even]
    inputs = (jacobian, states, harmonic_of_slot, coupling)
    part, table, sums, held_harm, held_coup = call(
        first_kernel,
        (
            shaped(shape, F32),
            shaped((padded, 128), F32),
            shaped((padded // 2, 128), F32),
            pltpu.SMEM(harmonic_of_slot.shape, jnp.int32),
            pltpu.SMEM(coupling.shape, jnp.int32),
        ),
        [HBM] * 4,
        work,
        [
            pltpu.VMEM((padded, 128), jacobian.dtype),
            pltpu.VMEM(shape, states.dtype),
            dma((PIECES,)),
            dma((3,)),
        ],
    )(*[pltpu.with_memory_space_constraint(x, HBM) for x in inputs])

    def more(groups, blocks, part, dtype):
        return call(
            functools.partial(next_kernel, groups),
            shaped(shape, dtype),
            [SMEM] * 2 + [VMEM] * (len(groups) + 3),
            work * len(groups),
        )(held_harm, held_coup, *blocks, table, sums, part)

    part = more([1], [partner], part, F32)
    *even_states, part = lax.optimization_barrier((*even_states, part))
    odd_states = [swap(block, 1) for block in even_states]

    part = more(even, even_states, part, F32)
    flux = more(odd, odd_states, part, states.dtype)
    near = lax.ppermute(flux, "gx", [(i, i ^ 1) for i in range(planes)])
    far = lax.ppermute(
        flux, "gx", [(i, (i + 1) % planes if i % 2 else (i - 1) % planes) for i in range(planes)]
    )
    sources = cells * VARS * VARS
    local = call(
        functools.partial(local_kernel, coupling.shape[0]),
        shaped(shape, F32),
        [SMEM] + [VMEM] * 3,
        work // 4,
        [pltpu.VMEM((-(-sources // 8) * 8 + 8, 128), F32)],
    )(held_harm, flux, states, source.reshape(sources, 128))
    return call(final_kernel, shaped(shape, states.dtype), [VMEM] * 3, work // 8)(local, near, far)


def solution(mesh):
    return jax.shard_map(
        body,
        mesh=mesh,
        in_specs=(
            P("harm", "gx", None, None, None, None),
            P(None, "gx", None, None, None, None),
            P("gx", None, None, None),
            P(),
            P(),
        ),
        out_specs=P("harm", "gx", None, None, None, None),
        check_vma=False,
    )
```

time: 35.1 us -> 21.8 us (0.62)
  local copies, waits for them, and re-layouts: 5.67 us -> 0.03 us
  Pallas kernels: 11.5 us -> 5.87 us
  waiting for transfers between devices: 9.41 us -> 7.29 us
    pallas_call x3 -> x6, Pallas kernels: 11.5 us -> 5.87 us  [the longest x3 2.67 us: more(): call(functools.partial(next_kernel, groups), shaped(shape, dtype), [SMEM]...]
    reshape x2 -> x1, local copies, waits for them, and re-layouts: 3.64 us -> 0.02 us  [body(): source.reshape(sources, 128)]
    unnamed x13 -> x5, local copies, waits for them, and re-layouts: 2.02 us -> 0.02 us
    ppermute x3, waiting for transfers between devices: 4.41 us -> 2.42 us  [swap(): return lax.ppermute(block, 'harm', [(i, i ^ shift) for i in range(harms)])]
  transfers between devices with their start and end apart: 5 -> 5, of which waited for: 3 -> 4; matrix products, arithmetic and copies ran while one was open for 10% -> 0% of each run, Pallas kernels for 14% -> 19%
where the time goes in v2:
time: 21.8 us; the launch traced here: 21.6 us
  starting transfers between devices  8.35 us (38%)
  waiting for transfers between devices  7.29 us (33%)
  Pallas kernels  5.87 us (27%)
    ppermute x1, starting transfers between devices, body(): lax.ppermute(flux, 'gx', [(i, (i + 1) % planes if i % 2 else (i - 1) % pl...  3.54 us
    ppermute x1, waiting for transfers between devices, body(): near = lax.ppermute(flux, 'gx', [(i, i ^ 1) for i in range(planes)])  3.48 us
    ppermute x3, starting transfers between devices, swap(): return lax.ppermute(block, 'harm', [(i, i ^ shift) for i in range(harms)])  2.97 us
    pallas_call x3, Pallas kernels, more(): call(functools.partial(next_kernel, groups), shaped(shape, dtype), [SMEM]...  2.67 us
    ppermute x3, waiting for transfers between devices, swap(): return lax.ppermute(block, 'harm', [(i, i ^ shift) for i in range(harms)])  2.42 us
    pallas_call x1, Pallas kernels, body(): call(first_kernel, (shaped(shape, F32), shaped((padded, 128), F32), shape...  2.22 us
    ppermute x1, starting transfers between devices, body(): near = lax.ppermute(flux, 'gx', [(i, i ^ 1) for i in range(planes)])  1.84 us
    ppermute x1, waiting for transfers between devices, body(): lax.ppermute(flux, 'gx', [(i, (i + 1) % planes if i % 2 else (i - 1) % pl...  1.39 us
  transfers between devices with their start and end apart: 5, of which 4 were waited for; matrix products, arithmetic and copies ran while one was open for 0% of the time, Pallas kernels for 19%

profile of v2, /device:TPU:0, one launch (start us, length us, event | category | flops | bytes accessed | tf_op | source)
XLA Modules:
  0.0 21.6 jit_solution(2646132270059706647)
XLA Ops:
  0.0 0.5 %collective-permute-start.1 = (bf16[4,2,5,2,8,128]{5,4,3,2,1,0:T(8,128)(2,1)}, bf16[4,2,5,2,8,128]{5,4,3,2,1,0:T(8,128)(2,1)S(1)}, u32[]{:S(2)}, u32[]{:S(2)}) collective-permute-start(bf16[4,2,5,2,8,128]{5,4,3,2,1,0:T(8,128)(2,1)} %state_ref.1), channel_id=1, source_target_pairs={{0,8},{8,0},{16,24},{24,16},{1,9},{9,1},{17,25},{25,17},{2,10},{10... | collective-permute-start | bytes 491528 | tf_op jit(solution)/shard_map/ppermute | solution.py:201
  0.5 2.5 %collective-permute-start = (bf16[4,2,5,2,8,128]{5,4,3,2,1,0:T(8,128)(2,1)}, bf16[4,2,5,2,8,128]{5,4,3,2,1,0:T(8,128)(2,1)S(1)}, u32[]{:S(2)}, u32[]{:S(2)}) collective-permute-start(bf16[4,2,5,2,8,128]{5,4,3,2,1,0:T(8,128)(2,1)} %state_ref.1), channel_id=1, source_target_pairs={{0,16},{8,24},{16,0},{24,8},{1,17},{9,25},{17,1},{25,9},{2,18},{10... | collective-permute-start | bytes 491528 | tf_op jit(solution)/shard_map/ppermute | solution.py:201
  3.0 2.2 %shard_map.55 = (f32[4,2,5,2,8,128]{5,4,3,2,1,0:T(8,128)S(1)}, f32[3104,128]{1,0:T(8,128)S(1)}, f32[1552,128]{1,0:T(8,128)S(1)}, s32[16]{0:T(128)S(4)}, s32[16,16]{1,0:T(8,128)S(4)}) custom-call(bf16[31,2,5,5,2,128]{5,4,3,2,1,0:T(2,128)(2,1)} %jac_hbm.1, bf16[4,2,5,2,8,128]{5,4,3,2,1,0:T(8,128)(2,1)} %state_ref.1, s32[16]{0:T(128)} %harm_hbm.1, ...), custom_call_target="tpu_custom_call" | custom-call | flops 9830400 | tf_op jit(solution)/shard_map/pallas_call | solution.py:209
  5.2 0.0 collective-permute-done.1.refs_0_
  5.2 0.9 %shard_map.56.refs_3_ = f32[4,2,5,2,8,128]{5,4,3,2,1,0:T(8,128)S(1)} custom-call(s32[16]{0:T(128)S(4)} %get-tuple-element.12.harm_ref, s32[16,16]{1,0:T(8,128)S(4)} %get-tuple-element.13.coup_ref, bf16[4,2,5,2,8,128]{5,4,3,2,1,0:T(8,128)(2,1)S(1)} %collective-permute-done.1.refs_0_, f32[3104,128]{1,0:T(8,128)S(1)} %get-tuple-element.14.refs_1_, ...), custom_call_target="tpu_custom_call" | custom-call | flops 9830400 | tf_op jit(solution)/shard_map/pallas_call | solution.py:229
  6.1 1.9 %collective-permute-done.refs_0_ = bf16[4,2,5,2,8,128]{5,4,3,2,1,0:T(8,128)(2,1)S(1)} collective-permute-done((bf16[4,2,5,2,8,128]{5,4,3,2,1,0:T(8,128)(2,1)}, bf16[4,2,5,2,8,128]{5,4,3,2,1,0:T(8,128)(2,1)S(1)}, u32[]{:S(2)}, u32[]{:S(2)}) %collective-permute-start) | collective-permute-done | bytes 163872 | tf_op jit(solution)/shard_map/ppermute | solution.py:201
  8.1 0.0 collective-permute-start.2
  8.1 0.9 %shard_map.57.refs_3_ = f32[4,2,5,2,8,128]{5,4,3,2,1,0:T(8,128)S(1)} custom-call(s32[16]{0:T(128)S(4)} %get-tuple-element.12.harm_ref, s32[16,16]{1,0:T(8,128)S(4)} %get-tuple-element.13.coup_ref, bf16[4,2,5,2,8,128]{5,4,3,2,1,0:T(8,128)(2,1)S(1)} %collective-permute-done.refs_0_, f32[3104,128]{1,0:T(8,128)S(1)} %get-tuple-element.14.refs_1_, ...), custom_call_target="tpu_custom_call" | custom-call | flops 9830400 | tf_op jit(solution)/shard_map/pallas_call | solution.py:229
  8.9 0.0 copy-start.1
  9.0 0.0 copy-start
  9.0 0.5 %collective-permute-done.2.refs_0_ = bf16[4,2,5,2,8,128]{5,4,3,2,1,0:T(8,128)(2,1)S(1)} collective-permute-done((bf16[4,2,5,2,8,128]{5,4,3,2,1,0:T(8,128)(2,1)S(1)}, bf16[4,2,5,2,8,128]{5,4,3,2,1,0:T(8,128)(2,1)S(1)}, u32[]{:S(2)}, u32[]{:S(2)}) %collective-permute-start.2) | collective-permute-done | bytes 163872 | tf_op jit(solution)/shard_map/ppermute | solution.py:201
  9.4 0.9 %shard_map.58.flux_ref = bf16[4,2,5,2,8,128]{5,4,3,2,1,0:T(8,128)(2,1)S(1)} custom-call(s32[16]{0:T(128)S(4)} %get-tuple-element.12.harm_ref, s32[16,16]{1,0:T(8,128)S(4)} %get-tuple-element.13.coup_ref, bf16[4,2,5,2,8,128]{5,4,3,2,1,0:T(8,128)(2,1)S(1)} %collective-permute-done.2.refs_0_, f32[3104,128]{1,0:T(8,128)S(1)} %get-tuple-element.14.refs_1_, ...), custom_call_target="tpu_custom_call" | custom-call | flops 9830400 | tf_op jit(solution)/shard_map/pallas_call | solution.py:229
  10.3 1.8 %collective-permute-start.3 = (bf16[4,2,5,2,8,128]{5,4,3,2,1,0:T(8,128)(2,1)S(1)}, bf16[4,2,5,2,8,128]{5,4,3,2,1,0:T(8,128)(2,1)S(1)}, u32[]{:S(2)}, u32[]{:S(2)}) collective-permute-start(bf16[4,2,5,2,8,128]{5,4,3,2,1,0:T(8,128)(2,1)S(1)} %shard_map.58.flux_ref), channel_id=1, source_target_pairs={{0,1},{1,0},{2,3},{3,2},{4,5},{5,4},{6,7},{7,6},{8,9},{9,8},{10,11... | collective-permute-start | bytes 491528 | tf_op jit(solution)/shard_map/ppermute | solution.py:242
  12.2 3.5 %collective-permute-start.4 = (bf16[4,2,5,2,8,128]{5,4,3,2,1,0:T(8,128)(2,1)S(1)}, bf16[4,2,5,2,8,128]{5,4,3,2,1,0:T(8,128)(2,1)S(1)}, u32[]{:S(2)}, u32[]{:S(2)}) collective-permute-start(bf16[4,2,5,2,8,128]{5,4,3,2,1,0:T(8,128)(2,1)S(1)} %shard_map.58.flux_ref), channel_id=1, source_target_pairs={{0,7},{1,2},{2,1},{3,4},{4,3},{5,6},{6,5},{7,0},{8,15},{9,10},{10,... | collective-permute-start | bytes 491528 | tf_op jit(solution)/shard_map/ppermute | solution.py:243
  15.7 0.0 copy-done.1
  15.8 0.0 copy-done
  15.8 0.2 shard_map.59.local_ref
  16.0 3.5 %collective-permute-done.3.near_ref = bf16[4,2,5,2,8,128]{5,4,3,2,1,0:T(8,128)(2,1)S(1)} collective-permute-done((bf16[4,2,5,2,8,128]{5,4,3,2,1,0:T(8,128)(2,1)S(1)}, bf16[4,2,5,2,8,128]{5,4,3,2,1,0:T(8,128)(2,1)S(1)}, u32[]{:S(2)}, u32[]{:S(2)}) %collective-permute-start.3) | collective-permute-done | bytes 163872 | tf_op jit(solution)/shard_map/ppermute | solution.py:242
  19.5 1.4 %collective-permute-done.4.far_ref = bf16[4,2,5,2,8,128]{5,4,3,2,1,0:T(8,128)(2,1)S(1)} collective-permute-done((bf16[4,2,5,2,8,128]{5,4,3,2,1,0:T(8,128)(2,1)S(1)}, bf16[4,2,5,2,8,128]{5,4,3,2,1,0:T(8,128)(2,1)S(1)}, u32[]{:S(2)}, u32[]{:S(2)}) %collective-permute-start.4) | collective-permute-done | bytes 163872 | tf_op jit(solution)/shard_map/ppermute | solution.py:243
  20.8 0.8 %shard_map.60 = bf16[4,2,5,2,8,128]{5,4,3,2,1,0:T(8,128)(2,1)} custom-call(f32[4,2,5,2,8,128]{5,4,3,2,1,0:T(8,128)S(1)} %shard_map.59.local_ref, bf16[4,2,5,2,8,128]{5,4,3,2,1,0:T(8,128)(2,1)S(1)} %collective-permute-done.3.near_ref, bf16[4,2,5,2,8,128]{5,4,3,2,1,0:T(8,128)(2,1)S(1)} %collective-permute-done.4.far_ref), custom_call_target="tpu_custom_call" | custom-call | flops 1228800 | tf_op jit(solution)/shard_map/pallas_call | solution.py:254
  (2 shorter events, 0.0 us)
Async XLA Ops:
  0.0 5.2 %collective-permute-start.1 = (bf16[4,2,5,2,8,128]{5,4,3,2,1,0:T(8,128)(2,1)}, bf16[4,2,5,2,8,128]{5,4,3,2,1,0:T(8,128)(2,1)S(1)}, u32[]{:S(2)}, u32[]{:S(2)}) collective-permute-start(bf16[4,2,5,2,8,128]{5,4,3,2,1,0:T(8,128)(2,1)} %state_ref.1), channel_id=1, source_target_pairs={{0,8},{8,0},{16,24},{24,16},{1,9},{9,1},{17,25},{25,17},{2,10},{10... | collective-permute-start | bytes 491528 | tf_op jit(solution)/shard_map/ppermute | solution.py:201
  0.5 7.6 %collective-permute-start = (bf16[4,2,5,2,8,128]{5,4,3,2,1,0:T(8,128)(2,1)}, bf16[4,2,5,2,8,128]{5,4,3,2,1,0:T(8,128)(2,1)S(1)}, u32[]{:S(2)}, u32[]{:S(2)}) collective-permute-start(bf16[4,2,5,2,8,128]{5,4,3,2,1,0:T(8,128)(2,1)} %state_ref.1), channel_id=1, source_target_pairs={{0,16},{8,24},{16,0},{24,8},{1,17},{9,25},{17,1},{25,9},{2,18},{10... | collective-permute-start | bytes 491528 | tf_op jit(solution)/shard_map/ppermute | solution.py:201
  8.1 1.4 %collective-permute-start.2 = (bf16[4,2,5,2,8,128]{5,4,3,2,1,0:T(8,128)(2,1)S(1)}, bf16[4,2,5,2,8,128]{5,4,3,2,1,0:T(8,128)(2,1)S(1)}, u32[]{:S(2)}, u32[]{:S(2)}) collective-permute-start(bf16[4,2,5,2,8,128]{5,4,3,2,1,0:T(8,128)(2,1)S(1)} %collective-permute-done.refs_0_), channel_id=1, source_target_pairs={{0,8},{8,0},{16,24},{24,16},{1,9},{9,1},{17,25},{25,17},{2,10},{10... | collective-permute-start | bytes 491528 | tf_op jit(solution)/shard_map/ppermute | solution.py:201
  8.9 6.8 %copy-start.1 = (bf16[2,5,5,128]{3,0,2,1:T(2,128)(2,1)S(1)}, bf16[2,5,5,128]{3,0,2,1:T(2,128)(2,1)}, u32[]{:S(2)}) copy-start(bf16[2,5,5,128]{3,0,2,1:T(2,128)(2,1)} %param.7) | copy-start | bytes 38404
  9.0 6.8 %copy-start = (bf16[4,2,5,2,8,128]{5,4,3,2,1,0:T(8,128)(2,1)S(1)}, bf16[4,2,5,2,8,128]{5,4,3,2,1,0:T(8,128)(2,1)}, u32[]{:S(2)}) copy-start(bf16[4,2,5,2,8,128]{5,4,3,2,1,0:T(8,128)(2,1)} %state_ref.1) | copy-start | bytes 491524
  10.3 9.1 %collective-permute-start.3 = (bf16[4,2,5,2,8,128]{5,4,3,2,1,0:T(8,128)(2,1)S(1)}, bf16[4,2,5,2,8,128]{5,4,3,2,1,0:T(8,128)(2,1)S(1)}, u32[]{:S(2)}, u32[]{:S(2)}) collective-permute-start(bf16[4,2,5,2,8,128]{5,4,3,2,1,0:T(8,128)(2,1)S(1)} %shard_map.58.flux_ref), channel_id=1, source_target_pairs={{0,1},{1,0},{2,3},{3,2},{4,5},{5,4},{6,7},{7,6},{8,9},{9,8},{10,11... | collective-permute-start | bytes 491528 | tf_op jit(solution)/shard_map/ppermute | solution.py:242
  12.2 8.7 %collective-permute-start.4 = (bf16[4,2,5,2,8,128]{5,4,3,2,1,0:T(8,128)(2,1)S(1)}, bf16[4,2,5,2,8,128]{5,4,3,2,1,0:T(8,128)(2,1)S(1)}, u32[]{:S(2)}, u32[]{:S(2)}) collective-permute-start(bf16[4,2,5,2,8,128]{5,4,3,2,1,0:T(8,128)(2,1)S(1)} %shard_map.58.flux_ref), channel_id=1, source_target_pairs={{0,7},{1,2},{2,1},{3,4},{4,3},{5,6},{6,5},{7,0},{8,15},{9,10},{10,... | collective-permute-start | bytes 491528 | tf_op jit(solution)/shard_map/ppermute | solution.py:243

commit v3 on v2

--- a/solution.py
+++ b/solution.py
@@ -145,11 +145,14 @@
     lax.fori_loop(0, own_count, body, 0)
 
 
-def final_kernel(local_ref, near_ref, far_ref, out_ref):
+def final_kernel(local_ref, near_ref, far_ref, out_hbm, out_ref, sem):
     own_count, cells = out_ref.shape[:2]
 
+    def put(slot):
+        return pltpu.make_async_copy(out_ref.at[slot], out_hbm.at[slot], sem.at[slot])
+
     def finish(left_ref, right_ref):
-        def body(slot, _):
+        for slot in range(own_count):
             for a in range(VARS):
                 for cell in range(cells):
                     total = local_ref[slot, cell, a]
@@ -160,9 +163,7 @@
                         elif place >= cells:
                             total = total + weight * right_ref[slot, place - cells, a].astype(F32)
                     out_ref[slot, cell, a] = total.astype(out_ref.dtype)
-            return 0
-
-        lax.fori_loop(0, own_count, body, 0)
+            put(slot).start()
 
     even = lax.axis_index("gx") % 2 == 0
 
@@ -173,6 +174,9 @@
     @pl.when(jnp.logical_not(even))
     def _():
         finish(near_ref, far_ref)
+
+    for slot in range(own_count):
+        put(slot).wait()
 
 
 def call(kernel, out, spaces, flops, scratch=()):
@@ -251,7 +255,13 @@
         work // 4,
         [pltpu.VMEM((-(-sources // 8) * 8 + 8, 128), F32)],
     )(held_harm, flux, states, source.reshape(sources, 128))
-    return call(final_kernel, shaped(shape, states.dtype), [VMEM] * 3, work // 8)(local, near, far)
+    return call(
+        final_kernel,
+        HBM(shape, states.dtype),
+        [VMEM] * 3,
+        work // 8,
+        [pltpu.VMEM(shape, states.dtype), dma((own_count,))],
+    )(local, near, far)
 
 
 def solution(mesh):

time: 21.8 us -> 21.7 us (level)
  no operation moved by 1% of the time
where the time goes in v3:
time: 21.7 us; the launch traced here: 21.6 us
  starting transfers between devices  8.35 us (38%)
  waiting for transfers between devices  7.29 us (34%)
  Pallas kernels  5.83 us (27%)
    ppermute x1, starting transfers between devices, body(): lax.ppermute(flux, 'gx', [(i, (i + 1) % planes if i % 2 else (i - 1) % pl...  3.54 us
    ppermute x1, waiting for transfers between devices, body(): near = lax.ppermute(flux, 'gx', [(i, i ^ 1) for i in range(planes)])  3.48 us
    ppermute x3, starting transfers between devices, swap(): return lax.ppermute(block, 'harm', [(i, i ^ shift) for i in range(harms)])  2.97 us
    pallas_call x3, Pallas kernels, more(): call(functools.partial(next_kernel, groups), shaped(shape, dtype), [SMEM]...  2.67 us
    ppermute x3, waiting for transfers between devices, swap(): return lax.ppermute(block, 'harm', [(i, i ^ shift) for i in range(harms)])  2.42 us
    pallas_call x1, Pallas kernels, body(): call(first_kernel, (shaped(shape, F32), shaped((padded, 128), F32), shape...  2.22 us
    ppermute x1, starting transfers between devices, body(): near = lax.ppermute(flux, 'gx', [(i, i ^ 1) for i in range(planes)])  1.84 us
    ppermute x1, waiting for transfers between devices, body(): lax.ppermute(flux, 'gx', [(i, (i + 1) % planes if i % 2 else (i - 1) % pl...  1.39 us
  transfers between devices with their start and end apart: 5, of which 4 were waited for; matrix products, arithmetic and copies ran while one was open for 0% of the time, Pallas kernels for 19%

profile of v3, /device:TPU:0, one launch (start us, length us, event | category | flops | bytes accessed | tf_op | source)
XLA Modules:
  0.0 21.6 jit_solution(9571815095399134076)
XLA Ops:
  0.0 0.5 %collective-permute-start.1 = (bf16[4,2,5,2,8,128]{5,4,3,2,1,0:T(8,128)(2,1)}, bf16[4,2,5,2,8,128]{5,4,3,2,1,0:T(8,128)(2,1)S(1)}, u32[]{:S(2)}, u32[]{:S(2)}) collective-permute-start(bf16[4,2,5,2,8,128]{5,4,3,2,1,0:T(8,128)(2,1)} %state_ref.1), channel_id=1, source_target_pairs={{0,8},{8,0},{16,24},{24,16},{1,9},{9,1},{17,25},{25,17},{2,10},{10... | collective-permute-start | bytes 491528 | tf_op jit(solution)/shard_map/ppermute | solution.py:205
  0.5 2.5 %collective-permute-start = (bf16[4,2,5,2,8,128]{5,4,3,2,1,0:T(8,128)(2,1)}, bf16[4,2,5,2,8,128]{5,4,3,2,1,0:T(8,128)(2,1)S(1)}, u32[]{:S(2)}, u32[]{:S(2)}) collective-permute-start(bf16[4,2,5,2,8,128]{5,4,3,2,1,0:T(8,128)(2,1)} %state_ref.1), channel_id=1, source_target_pairs={{0,16},{8,24},{16,0},{24,8},{1,17},{9,25},{17,1},{25,9},{2,18},{10... | collective-permute-start | bytes 491528 | tf_op jit(solution)/shard_map/ppermute | solution.py:205
  3.0 2.2 %shard_map.55 = (f32[4,2,5,2,8,128]{5,4,3,2,1,0:T(8,128)S(1)}, f32[3104,128]{1,0:T(8,128)S(1)}, f32[1552,128]{1,0:T(8,128)S(1)}, s32[16]{0:T(128)S(4)}, s32[16,16]{1,0:T(8,128)S(4)}) custom-call(bf16[31,2,5,5,2,128]{5,4,3,2,1,0:T(2,128)(2,1)} %jac_hbm.1, bf16[4,2,5,2,8,128]{5,4,3,2,1,0:T(8,128)(2,1)} %state_ref.1, s32[16]{0:T(128)} %harm_hbm.1, ...), custom_call_target="tpu_custom_call" | custom-call | flops 9830400 | tf_op jit(solution)/shard_map/pallas_call | solution.py:213
  5.2 0.0 collective-permute-done.1.refs_0_
  5.2 0.9 %shard_map.56.refs_3_ = f32[4,2,5,2,8,128]{5,4,3,2,1,0:T(8,128)S(1)} custom-call(s32[16]{0:T(128)S(4)} %get-tuple-element.12.harm_ref, s32[16,16]{1,0:T(8,128)S(4)} %get-tuple-element.13.coup_ref, bf16[4,2,5,2,8,128]{5,4,3,2,1,0:T(8,128)(2,1)S(1)} %collective-permute-done.1.refs_0_, f32[3104,128]{1,0:T(8,128)S(1)} %get-tuple-element.14.refs_1_, ...), custom_call_target="tpu_custom_call" | custom-call | flops 9830400 | tf_op jit(solution)/shard_map/pallas_call | solution.py:233
  6.1 1.9 %collective-permute-done.refs_0_ = bf16[4,2,5,2,8,128]{5,4,3,2,1,0:T(8,128)(2,1)S(1)} collective-permute-done((bf16[4,2,5,2,8,128]{5,4,3,2,1,0:T(8,128)(2,1)}, bf16[4,2,5,2,8,128]{5,4,3,2,1,0:T(8,128)(2,1)S(1)}, u32[]{:S(2)}, u32[]{:S(2)}) %collective-permute-start) | collective-permute-done | bytes 163872 | tf_op jit(solution)/shard_map/ppermute | solution.py:205
  8.1 0.0 collective-permute-start.2
  8.1 0.9 %shard_map.57.refs_3_ = f32[4,2,5,2,8,128]{5,4,3,2,1,0:T(8,128)S(1)} custom-call(s32[16]{0:T(128)S(4)} %get-tuple-element.12.harm_ref, s32[16,16]{1,0:T(8,128)S(4)} %get-tuple-element.13.coup_ref, bf16[4,2,5,2,8,128]{5,4,3,2,1,0:T(8,128)(2,1)S(1)} %collective-permute-done.refs_0_, f32[3104,128]{1,0:T(8,128)S(1)} %get-tuple-element.14.refs_1_, ...), custom_call_target="tpu_custom_call" | custom-call | flops 9830400 | tf_op jit(solution)/shard_map/pallas_call | solution.py:233
  8.9 0.0 copy-start.1
  9.0 0.0 copy-start
  9.0 0.5 %collective-permute-done.2.refs_0_ = bf16[4,2,5,2,8,128]{5,4,3,2,1,0:T(8,128)(2,1)S(1)} collective-permute-done((bf16[4,2,5,2,8,128]{5,4,3,2,1,0:T(8,128)(2,1)S(1)}, bf16[4,2,5,2,8,128]{5,4,3,2,1,0:T(8,128)(2,1)S(1)}, u32[]{:S(2)}, u32[]{:S(2)}) %collective-permute-start.2) | collective-permute-done | bytes 163872 | tf_op jit(solution)/shard_map/ppermute | solution.py:205
  9.4 0.9 %shard_map.58.flux_ref = bf16[4,2,5,2,8,128]{5,4,3,2,1,0:T(8,128)(2,1)S(1)} custom-call(s32[16]{0:T(128)S(4)} %get-tuple-element.12.harm_ref, s32[16,16]{1,0:T(8,128)S(4)} %get-tuple-element.13.coup_ref, bf16[4,2,5,2,8,128]{5,4,3,2,1,0:T(8,128)(2,1)S(1)} %collective-permute-done.2.refs_0_, f32[3104,128]{1,0:T(8,128)S(1)} %get-tuple-element.14.refs_1_, ...), custom_call_target="tpu_custom_call" | custom-call | flops 9830400 | tf_op jit(solution)/shard_map/pallas_call | solution.py:233
  10.3 1.8 %collective-permute-start.3 = (bf16[4,2,5,2,8,128]{5,4,3,2,1,0:T(8,128)(2,1)S(1)}, bf16[4,2,5,2,8,128]{5,4,3,2,1,0:T(8,128)(2,1)S(1)}, u32[]{:S(2)}, u32[]{:S(2)}) collective-permute-start(bf16[4,2,5,2,8,128]{5,4,3,2,1,0:T(8,128)(2,1)S(1)} %shard_map.58.flux_ref), channel_id=1, source_target_pairs={{0,1},{1,0},{2,3},{3,2},{4,5},{5,4},{6,7},{7,6},{8,9},{9,8},{10,11... | collective-permute-start | bytes 491528 | tf_op jit(solution)/shard_map/ppermute | solution.py:246
  12.2 3.5 %collective-permute-start.4 = (bf16[4,2,5,2,8,128]{5,4,3,2,1,0:T(8,128)(2,1)S(1)}, bf16[4,2,5,2,8,128]{5,4,3,2,1,0:T(8,128)(2,1)S(1)}, u32[]{:S(2)}, u32[]{:S(2)}) collective-permute-start(bf16[4,2,5,2,8,128]{5,4,3,2,1,0:T(8,128)(2,1)S(1)} %shard_map.58.flux_ref), channel_id=1, source_target_pairs={{0,7},{1,2},{2,1},{3,4},{4,3},{5,6},{6,5},{7,0},{8,15},{9,10},{10,... | collective-permute-start | bytes 491528 | tf_op jit(solution)/shard_map/ppermute | solution.py:247
  15.7 0.0 copy-done.1
  15.8 0.0 copy-done
  15.8 0.2 shard_map.59.local_ref
  16.0 3.5 %collective-permute-done.3.near_ref = bf16[4,2,5,2,8,128]{5,4,3,2,1,0:T(8,128)(2,1)S(1)} collective-permute-done((bf16[4,2,5,2,8,128]{5,4,3,2,1,0:T(8,128)(2,1)S(1)}, bf16[4,2,5,2,8,128]{5,4,3,2,1,0:T(8,128)(2,1)S(1)}, u32[]{:S(2)}, u32[]{:S(2)}) %collective-permute-start.3) | collective-permute-done | bytes 163872 | tf_op jit(solution)/shard_map/ppermute | solution.py:246
  19.5 1.4 %collective-permute-done.4.far_ref = bf16[4,2,5,2,8,128]{5,4,3,2,1,0:T(8,128)(2,1)S(1)} collective-permute-done((bf16[4,2,5,2,8,128]{5,4,3,2,1,0:T(8,128)(2,1)S(1)}, bf16[4,2,5,2,8,128]{5,4,3,2,1,0:T(8,128)(2,1)S(1)}, u32[]{:S(2)}, u32[]{:S(2)}) %collective-permute-start.4) | collective-permute-done | bytes 163872 | tf_op jit(solution)/shard_map/ppermute | solution.py:247
  20.8 0.7 %shard_map.60 = bf16[4,2,5,2,8,128]{5,4,3,2,1,0:T(8,128)(2,1)} custom-call(f32[4,2,5,2,8,128]{5,4,3,2,1,0:T(8,128)S(1)} %shard_map.59.local_ref, bf16[4,2,5,2,8,128]{5,4,3,2,1,0:T(8,128)(2,1)S(1)} %collective-permute-done.3.near_ref, bf16[4,2,5,2,8,128]{5,4,3,2,1,0:T(8,128)(2,1)S(1)} %collective-permute-done.4.far_ref), custom_call_target="tpu_custom_call" | custom-call | flops 1228800 | tf_op jit(solution)/shard_map/pallas_call | solution.py:258
  (2 shorter events, 0.0 us)
Async XLA Ops:
  0.0 5.2 %collective-permute-start.1 = (bf16[4,2,5,2,8,128]{5,4,3,2,1,0:T(8,128)(2,1)}, bf16[4,2,5,2,8,128]{5,4,3,2,1,0:T(8,128)(2,1)S(1)}, u32[]{:S(2)}, u32[]{:S(2)}) collective-permute-start(bf16[4,2,5,2,8,128]{5,4,3,2,1,0:T(8,128)(2,1)} %state_ref.1), channel_id=1, source_target_pairs={{0,8},{8,0},{16,24},{24,16},{1,9},{9,1},{17,25},{25,17},{2,10},{10... | collective-permute-start | bytes 491528 | tf_op jit(solution)/shard_map/ppermute | solution.py:205
  0.5 7.6 %collective-permute-start = (bf16[4,2,5,2,8,128]{5,4,3,2,1,0:T(8,128)(2,1)}, bf16[4,2,5,2,8,128]{5,4,3,2,1,0:T(8,128)(2,1)S(1)}, u32[]{:S(2)}, u32[]{:S(2)}) collective-permute-start(bf16[4,2,5,2,8,128]{5,4,3,2,1,0:T(8,128)(2,1)} %state_ref.1), channel_id=1, source_target_pairs={{0,16},{8,24},{16,0},{24,8},{1,17},{9,25},{17,1},{25,9},{2,18},{10... | collective-permute-start | bytes 491528 | tf_op jit(solution)/shard_map/ppermute | solution.py:205
  8.1 1.4 %collective-permute-start.2 = (bf16[4,2,5,2,8,128]{5,4,3,2,1,0:T(8,128)(2,1)S(1)}, bf16[4,2,5,2,8,128]{5,4,3,2,1,0:T(8,128)(2,1)S(1)}, u32[]{:S(2)}, u32[]{:S(2)}) collective-permute-start(bf16[4,2,5,2,8,128]{5,4,3,2,1,0:T(8,128)(2,1)S(1)} %collective-permute-done.refs_0_), channel_id=1, source_target_pairs={{0,8},{8,0},{16,24},{24,16},{1,9},{9,1},{17,25},{25,17},{2,10},{10... | collective-permute-start | bytes 491528 | tf_op jit(solution)/shard_map/ppermute | solution.py:205
  8.9 6.8 %copy-start.1 = (bf16[2,5,5,128]{3,0,2,1:T(2,128)(2,1)S(1)}, bf16[2,5,5,128]{3,0,2,1:T(2,128)(2,1)}, u32[]{:S(2)}) copy-start(bf16[2,5,5,128]{3,0,2,1:T(2,128)(2,1)} %param.7) | copy-start | bytes 38404
  9.0 6.8 %copy-start = (bf16[4,2,5,2,8,128]{5,4,3,2,1,0:T(8,128)(2,1)S(1)}, bf16[4,2,5,2,8,128]{5,4,3,2,1,0:T(8,128)(2,1)}, u32[]{:S(2)}) copy-start(bf16[4,2,5,2,8,128]{5,4,3,2,1,0:T(8,128)(2,1)} %state_ref.1) | copy-start | bytes 491524
  10.3 9.1 %collective-permute-start.3 = (bf16[4,2,5,2,8,128]{5,4,3,2,1,0:T(8,128)(2,1)S(1)}, bf16[4,2,5,2,8,128]{5,4,3,2,1,0:T(8,128)(2,1)S(1)}, u32[]{:S(2)}, u32[]{:S(2)}) collective-permute-start(bf16[4,2,5,2,8,128]{5,4,3,2,1,0:T(8,128)(2,1)S(1)} %shard_map.58.flux_ref), channel_id=1, source_target_pairs={{0,1},{1,0},{2,3},{3,2},{4,5},{5,4},{6,7},{7,6},{8,9},{9,8},{10,11... | collective-permute-start | bytes 491528 | tf_op jit(solution)/shard_map/ppermute | solution.py:246
  12.2 8.7 %collective-permute-start.4 = (bf16[4,2,5,2,8,128]{5,4,3,2,1,0:T(8,128)(2,1)S(1)}, bf16[4,2,5,2,8,128]{5,4,3,2,1,0:T(8,128)(2,1)S(1)}, u32[]{:S(2)}, u32[]{:S(2)}) collective-permute-start(bf16[4,2,5,2,8,128]{5,4,3,2,1,0:T(8,128)(2,1)S(1)} %shard_map.58.flux_ref), channel_id=1, source_target_pairs={{0,7},{1,2},{2,1},{3,4},{4,3},{5,6},{6,5},{7,0},{8,15},{9,10},{10,... | collective-permute-start | bytes 491528 | tf_op jit(solution)/shard_map/ppermute | solution.py:247
